TPU v7x, 512 devices: a whole 4x4x16 slice. The times are simulated.
512 devices in a mesh: swath: 32 (over z, core), chan: 16 (over x, y).
Axes of the slice: x: 4, y: 4, z: 16, core: 2. Of those that a mesh axis runs over, the one named last changes fastest.
Arguments:
- grid_profiles: bfloat16 [32768, 256], P('swath'), may hold values from -6 to 6
- send_lists: int32 [32, 32, 128], P('swath'), may hold values from 0 to 1023
- counts: int32 [32, 32], P('swath'), may hold values from 1 to 128, as said below
- angle_index: int32 [128], replicated, may hold values from 0 to 7
- jacobian: bfloat16 [3, 256, 608], P(None, None, 'chan'), may hold values from -0.375 to 0.375
- observed: bfloat16 [608, 131072], P('chan', 'swath'), may hold values from -6 to 6
- kappa: float32 [2, 608], P(None, 'chan'), may hold values from 0.04 to 0.24
- factor: bfloat16 [608, 608], P('chan')
Outputs:
- weighted: float32 [608, 131072], P('chan', 'swath')
Inputs may be any that keep to these rules, and one draw needn't show every extreme that they name: `counts`: some receiver gets 128 live slots from every sender; every entry is at least one.
All inputs are finite; a program needn't handle non-finite values.
Results may differ from a plain program's by a relative error of at most 0.0029.
Values may be sent and summed in bfloat16 or wider, within the bound.
A program may use at most 64 MiB of HBM per device.

v0:
```python
import math
import jax
import jax.numpy as jnp
from jax import lax
from jax.sharding import PartitionSpec as P

XTRACK = 128
NANG = 8
max_zenith = math.pi / 3.0


def extended_2(block, sides, width):
    for axis, dim in sides:
        count = lax.axis_size(axis)
        forward = [(i, i + 1) for i in range(count - 1)]
        backward = [(target, source) for source, target in forward]
        low = lax.ppermute(
            lax.slice_in_dim(block, block.shape[dim] - width, None, axis=dim), axis, forward
        )
        high = lax.ppermute(lax.slice_in_dim(block, 0, width, axis=dim), axis, backward)
        block = jnp.concatenate([low, block, high], axis=dim)
    return block


def diffuse_once(extended, along_rate, cross_rate):
    center = extended[:, 1:-1]
    along_sum = extended[:, 2:] + extended[:, :-2] - 2.0 * center
    side_pad = jnp.pad(center, ((0, 0), (0, 0), (1, 1)))
    cross_sum = side_pad[:, :, 2:] + side_pad[:, :, :-2] - 2.0 * center
    return center + along_rate * along_sum + cross_rate * cross_sum


def line_rims(smooth_field):
    return extended_2(smooth_field, (("swath", 1),), 1)


def on_device(grid_profiles, send_lists, counts, angle_index, jacobian, observed, kappa, factor):
    slot_rows = send_lists[0]
    slots = slot_rows.shape[1]
    own_chan = observed.shape[0]
    pixel_count = observed.shape[1]
    line_count = pixel_count // XTRACK
    live_slot = jnp.arange(slots, dtype=jnp.int32)[None, :] < counts[0][:, None]
    zero_value = jnp.zeros((), grid_profiles.dtype)
    outgoing = jnp.where(live_slot[:, :, None], grid_profiles[slot_rows], zero_value)
    incoming = lax.all_to_all(outgoing, "swath", split_axis=0, concat_axis=0, tiled=True)
    pixel_profiles = incoming.reshape(pixel_count, grid_profiles.shape[1])
    model = jnp.einsum("mkc,pk->mcp", jacobian, pixel_profiles, preferred_element_type=jnp.float32)
    zenith = angle_index.astype(jnp.float32) * (max_zenith / (NANG - 1))
    slant_path = 1.0 / jnp.cos(zenith) - 1.0
    model = model.reshape(3, own_chan, line_count, XTRACK)
    departure = observed.astype(jnp.float32).reshape(own_chan, line_count, XTRACK) - (
        model[0] + slant_path * model[1] + slant_path * slant_path * model[2]
    )
    along_rate = kappa[0][:, None, None]
    cross_rate = kappa[1][:, None, None]
    smooth_field = departure
    for sweep in range(3):
        smooth_field = diffuse_once(line_rims(smooth_field), along_rate, cross_rate)
    smoothed = smooth_field.reshape(own_chan, pixel_count).astype(jnp.bfloat16)
    return jnp.dot(
        factor,
        lax.all_gather(smoothed, "chan", axis=0, tiled=True),
        preferred_element_type=jnp.float32,
    )


def solution(mesh):
    in_specs = (
        P("swath", None),
        P("swath", None, None),
        P("swath", None),
        P(),
        P(None, None, "chan"),
        P("chan", "swath"),
        P(None, "chan"),
        P("chan", None),
    )
    out_specs = P("chan", "swath")
    return jax.shard_map(
        on_device, mesh=mesh, in_specs=in_specs, out_specs=out_specs, check_vma=False
    )
```

profile of v0, /device:TPU:1, one launch (start us, length us, event | category | flops | bytes accessed | tf_op | source)
XLA Modules:
  0.0 252.0 jit_solution(1715933017502331585)
XLA Ops:
  6.5 0.0 copy-start
  6.5 0.8 iota_compare_fusion
  7.3 0.7 fusion.29
  8.0 0.0 copy-done
  8.1 14.6 %gather_fusion = bf16[4096,256]{1,0:T(8,128)(2,1)S(1)} fusion(bf16[1024,256]{1,0:T(8,128)(2,1)S(1)} %copy-done, s32[4096]{0:T(1024)S(1)} %fusion.29), kind=kCustom, calls=%fused_computation | custom fusion | bytes 4210688 | tf_op jit(solution)/shard_map/gather | solution.py:45
  22.7 1.7 broadcast_select_fusion
  24.4 0.0 copy-start.1
  24.4 16.9 %all-to-all-start = ((bf16[32,128,256]{2,1,0:T(8,128)(2,1)}), bf16[32,128,256]{2,1,0:T(8,128)(2,1)S(1)}, u32[]{:S(2)}, u32[]{:S(2)}) async-start(bf16[32,128,256]{2,1,0:T(8,128)(2,1)} %broadcast_select_fusion), calls=%async_computation | async-start | bytes 4194304 | tf_op jit(solution)/shard_map/all_to_all | solution.py:46
  41.2 0.0 copy-start.5
  41.3 0.0 copy-start.2
  41.3 0.0 all-gather.3.cloned.1.call-start
  41.3 0.0 copy-done.1
  41.4 0.1 copy.9
  41.5 0.4 copy-done.5
  42.0 97.9 %all-to-all-done = bf16[32,128,256]{2,1,0:T(8,128)(2,1)S(1)} async-done(((bf16[32,128,256]{2,1,0:T(8,128)(2,1)}), bf16[32,128,256]{2,1,0:T(8,128)(2,1)S(1)}, u32[]{:S(2)}, u32[]{:S(2)}) %all-to-all-start) | async-done | bytes 2097184 | tf_op jit(solution)/shard_map/all_to_all | solution.py:46
  139.9 0.0 copy-done.2
  139.9 0.8 convolution_bitcast_fusion
  140.7 0.2 fusion.31
  140.8 0.1 copy.10
  141.0 0.1 copy.12
  141.1 0.0 copy-start.4
  141.1 0.1 copy.11
  141.2 0.3 fusion.14
  141.6 2.8 %collective-permute-start = (f32[38,1,128]{2,1,0:T(1,128)S(1)}, f32[38,1,128]{2,1,0:T(1,128)S(1)}, u32[]{:S(2)}, u32[]{:S(2)}) collective-permute-start(f32[38,1,128]{2,1,0:T(1,128)S(1)} %get-tuple-element.14), channel_id=1, source_target_pairs={{16,0},{32,16},{48,32},{64,48},{80,64},{96,80},{112,96},{128,112},... | collective-permute-start | bytes 58376 | tf_op jit(solution)/shard_map/ppermute | solution.py:20
  144.3 4.2 %collective-permute-start.1 = (f32[38,1,128]{2,1,0:T(1,128)S(1)}, f32[38,1,128]{2,1,0:T(1,128)S(1)}, u32[]{:S(2)}, u32[]{:S(2)}) collective-permute-start(f32[38,1,128]{2,1,0:T(1,128)S(1)} %get-tuple-element.15), channel_id=1, source_target_pairs={{0,16},{16,32},{32,48},{48,64},{64,80},{80,96},{96,112},{112,128},... | collective-permute-start | bytes 58376 | tf_op jit(solution)/shard_map/ppermute | solution.py:17
  148.6 0.0 copy-done.4
  148.6 0.0 collective-permute-done
  148.6 0.8 collective-permute-done.1
  149.4 0.5 fusion.3
  150.0 1.9 collective-permute-start.2
  151.9 4.2 %collective-permute-start.3 = (f32[38,1,128]{2,1,0:T(1,128)S(1)}, f32[38,1,128]{2,1,0:T(1,128)S(1)}, u32[]{:S(2)}, u32[]{:S(2)}) collective-permute-start(f32[38,1,128]{2,1,0:T(1,128)S(1)} %get-tuple-element.13), channel_id=1, source_target_pairs={{0,16},{16,32},{32,48},{48,64},{64,80},{80,96},{96,112},{112,128},... | collective-permute-start | bytes 58376 | tf_op jit(solution)/shard_map/ppermute | solution.py:17
  156.2 0.0 collective-permute-done.2
  156.2 0.9 collective-permute-done.3
  157.0 0.5 fusion.7
  157.6 1.9 collective-permute-start.4
  159.5 4.2 %collective-permute-start.5 = (f32[38,1,128]{2,1,0:T(1,128)S(1)}, f32[38,1,128]{2,1,0:T(1,128)S(1)}, u32[]{:S(2)}, u32[]{:S(2)}) collective-permute-start(f32[38,1,128]{2,1,0:T(1,128)S(1)} %get-tuple-element.11), channel_id=1, source_target_pairs={{0,16},{16,32},{32,48},{48,64},{64,80},{80,96},{96,112},{112,128},... | collective-permute-start | bytes 58376 | tf_op jit(solution)/shard_map/ppermute | solution.py:17
  163.8 0.0 collective-permute-done.4
  163.8 0.9 collective-permute-done.5
  164.6 0.6 fusion.12
  165.2 0.9 reshape.88
  166.1 0.0 all-gather.3.cloned.1.call-update
  166.2 0.0 copy-start.3
  166.2 69.0 %all-gather.3.cloned.1.call-done = bf16[16,38,4096]{2,1,0:T(8,128)(2,1)} async-done(((bf16[1,38,4096]{2,1,0:T(8,128)(2,1)}), bf16[16,38,4096]{2,1,0:T(8,128)(2,1)}) %all-gather.3.cloned.1.call-update) | async-done | bytes 4980752 | tf_op jit(solution)/shard_map/all_gather | solution.py:63
  235.2 5.7 %reshape.89 = bf16[608,4096]{1,0:T(8,128)(2,1)} reshape(bf16[16,38,4096]{2,1,0:T(8,128)(2,1)} %all-gather.3.cloned.1.call-done) | data formatting | bytes 9961472
  240.9 0.0 copy-done.3
  240.9 4.2 %convolution_bitcast_fusion.1 = f32[38,4096]{1,0:T(8,128)} fusion(bf16[608,4096]{1,0:T(8,128)(2,1)} %reshape.89, bf16[38,608]{1,0:T(8,128)(2,1)S(1)} %copy-done.3), kind=kOutput, calls=%fused_computation.2 | convolution fusion | flops 189267968 | bytes 5649536 | tf_op jit(solution)/shard_map/dot_general | solution.py:61
  (6 shorter events, 0.2 us)
Async XLA Ops:
  6.5 1.5 copy-start
  24.4 17.0 %copy-start.1 = (bf16[38,4096]{1,0:T(8,128)(2,1)S(1)}, bf16[38,4096]{1,0:T(8,128)(2,1)}, u32[]{:S(2)}) copy-start(bf16[38,4096]{1,0:T(8,128)(2,1)} %param.13) | copy-start | bytes 933892
  24.4 115.5 %all-to-all-start = ((bf16[32,128,256]{2,1,0:T(8,128)(2,1)}), bf16[32,128,256]{2,1,0:T(8,128)(2,1)S(1)}, u32[]{:S(2)}, u32[]{:S(2)}) async-start(bf16[32,128,256]{2,1,0:T(8,128)(2,1)} %broadcast_select_fusion), calls=%async_computation | async-start | bytes 4194304 | tf_op jit(solution)/shard_map/all_to_all | solution.py:46
  41.2 0.7 copy-start.5
  41.3 98.6 %copy-start.2 = (bf16[3,256,38]{1,2,0:T(8,128)(2,1)S(1)}, bf16[3,256,38]{1,2,0:T(8,128)(2,1)}, u32[]{:S(2)}) copy-start(bf16[3,256,38]{1,2,0:T(8,128)(2,1)} %param.12) | copy-start | bytes 175108
  41.3 193.9 %all-gather.3.cloned.1.call-start = ((), (), s32[]{:S(2)}) async-start(), calls=%async_computation.1 | async-start | bytes 5570560 | tf_op jit(solution)/shard_map/all_gather | solution.py:63
  141.1 7.5 %copy-start.4 = (f32[2,38]{1,0:T(2,128)S(1)}, f32[2,38]{1,0:T(2,128)}, u32[]{:S(2)}) copy-start(f32[2,38]{1,0:T(2,128)} %param.14) | copy-start | bytes 916
  141.6 7.0 %collective-permute-start = (f32[38,1,128]{2,1,0:T(1,128)S(1)}, f32[38,1,128]{2,1,0:T(1,128)S(1)}, u32[]{:S(2)}, u32[]{:S(2)}) collective-permute-start(f32[38,1,128]{2,1,0:T(1,128)S(1)} %get-tuple-element.14), channel_id=1, source_target_pairs={{16,0},{32,16},{48,32},{64,48},{80,64},{96,80},{112,96},{128,112},... | collective-permute-start | bytes 58376 | tf_op jit(solution)/shard_map/ppermute | solution.py:20
  144.3 5.1 %collective-permute-start.1 = (f32[38,1,128]{2,1,0:T(1,128)S(1)}, f32[38,1,128]{2,1,0:T(1,128)S(1)}, u32[]{:S(2)}, u32[]{:S(2)}) collective-permute-start(f32[38,1,128]{2,1,0:T(1,128)S(1)} %get-tuple-element.15), channel_id=1, source_target_pairs={{0,16},{16,32},{32,48},{48,64},{64,80},{80,96},{96,112},{112,128},... | collective-permute-start | bytes 58376 | tf_op jit(solution)/shard_map/ppermute | solution.py:17
  150.0 6.1 %collective-permute-start.2 = (f32[38,1,128]{2,1,0:T(1,128)S(1)}, f32[38,1,128]{2,1,0:T(1,128)S(1)}, u32[]{:S(2)}, u32[]{:S(2)}) collective-permute-start(f32[38,1,128]{2,1,0:T(1,128)S(1)} %get-tuple-element.12), channel_id=1, source_target_pairs={{16,0},{32,16},{48,32},{64,48},{80,64},{96,80},{112,96},{128,112},... | collective-permute-start | bytes 58376 | tf_op jit(solution)/shard_map/ppermute | solution.py:20
  151.9 5.1 %collective-permute-start.3 = (f32[38,1,128]{2,1,0:T(1,128)S(1)}, f32[38,1,128]{2,1,0:T(1,128)S(1)}, u32[]{:S(2)}, u32[]{:S(2)}) collective-permute-start(f32[38,1,128]{2,1,0:T(1,128)S(1)} %get-tuple-element.13), channel_id=1, source_target_pairs={{0,16},{16,32},{32,48},{48,64},{64,80},{80,96},{96,112},{112,128},... | collective-permute-start | bytes 58376 | tf_op jit(solution)/shard_map/ppermute | solution.py:17
  157.6 6.1 %collective-permute-start.4 = (f32[38,1,128]{2,1,0:T(1,128)S(1)}, f32[38,1,128]{2,1,0:T(1,128)S(1)}, u32[]{:S(2)}, u32[]{:S(2)}) collective-permute-start(f32[38,1,128]{2,1,0:T(1,128)S(1)} %get-tuple-element.10), channel_id=1, source_target_pairs={{16,0},{32,16},{48,32},{64,48},{80,64},{96,80},{112,96},{128,112},... | collective-permute-start | bytes 58376 | tf_op jit(solution)/shard_map/ppermute | solution.py:20
  159.5 5.1 %collective-permute-start.5 = (f32[38,1,128]{2,1,0:T(1,128)S(1)}, f32[38,1,128]{2,1,0:T(1,128)S(1)}, u32[]{:S(2)}, u32[]{:S(2)}) collective-permute-start(f32[38,1,128]{2,1,0:T(1,128)S(1)} %get-tuple-element.11), channel_id=1, source_target_pairs={{0,16},{16,32},{32,48},{48,64},{64,80},{80,96},{96,112},{112,128},... | collective-permute-start | bytes 58376 | tf_op jit(solution)/shard_map/ppermute | solution.py:17
  166.2 74.8 %copy-start.3 = (bf16[38,608]{1,0:T(8,128)(2,1)S(1)}, bf16[38,608]{1,0:T(8,128)(2,1)}, u32[]{:S(2)}) copy-start(bf16[38,608]{1,0:T(8,128)(2,1)} %param.15) | copy-start | bytes 138628
Sparse Core Ops, SparseCore 0:
  166.3 68.8 all-gather.2
where the time goes:
time: 253 us; the launch traced here: 252 us
  waiting for transfers between devices  170 us (67%)
  starting transfers between devices  36.2 us (14%)
  local copies, waits for them, and re-layouts  22.4 us (9%)
  between operations  13.6 us (5%)
  other arithmetic  5.22 us (2%)
  matrix products  4.96 us (2%)
    all_to_all x1, waiting for transfers between devices, on_device(): lax.all_to_all(outgoing, 'swath', split_axis=0, concat_axis=0, tiled=True)  97.9 us
    all_gather x1, waiting for transfers between devices, on_device(): lax.all_gather(smoothed, 'chan', axis=0, tiled=True)  69 us
    all_to_all x1, starting transfers between devices, on_device(): lax.all_to_all(outgoing, 'swath', split_axis=0, concat_axis=0, tiled=True)  16.9 us
    gather x1, local copies, waits for them, and re-layouts, on_device(): grid_profiles[slot_rows]  14.6 us
    ppermute x3, starting transfers between devices, extended_2(): lax.ppermute(lax.slice_in_dim(block, block.shape[dim] - width, None, axis...  12.6 us
    unnamed x18, local copies, waits for them, and re-layouts  7.56 us
    ppermute x3, starting transfers between devices, extended_2(): lax.ppermute(lax.slice_in_dim(block, 0, width, axis=dim), axis, backward)  6.62 us
  transfers between devices with their start and end apart: 8, of which 5 were waited for; matrix products, arithmetic and copies ran while one was open for 0% of the time, Pallas kernels for 0%

commit v1 on v0

--- a/solution.py
+++ b/solution.py
@@ -3,10 +3,34 @@
 import jax.numpy as jnp
 from jax import lax
 from jax.sharding import PartitionSpec as P
+from jax.lax import axis_index, ppermute, psum
 
 XTRACK = 128
 NANG = 8
 max_zenith = math.pi / 3.0
+
+
+def launch_floor(vals, array_dim=0):
+    side_arr = psum(1, "chan")
+    y = axis_index("chan")
+    passed, tmp, d_next = (side_arr, y, vals.shape[array_dim])
+    heap = [(q, (q + 1) % passed) for q in range(passed)]
+    table = [(q, (q - 1) % passed) for q in range(passed)]
+    w2 = jnp.zeros(
+        (*vals.shape[:array_dim], passed * d_next, *vals.shape[array_dim + 1 :]), vals.dtype
+    )
+    w2 = lax.dynamic_update_slice_in_dim(w2, vals, tmp * d_next, axis=array_dim)
+    res = response = vals
+    reached = passed // 2
+    for w in [*range(1, reached + 1)]:
+        res = ppermute(res, "chan", heap)
+        w2 = lax.dynamic_update_slice_in_dim(w2, res, (tmp - w) % passed * d_next, axis=array_dim)
+        if w < passed - reached:
+            response = ppermute(response, axis_name="chan", perm=table)
+            w2 = lax.dynamic_update_slice_in_dim(
+                w2, response, (tmp + w) % passed * d_next, axis=array_dim
+            )
+    return w2
 
 
 def extended_2(block, sides, width):
@@ -58,11 +82,7 @@
     for sweep in range(3):
         smooth_field = diffuse_once(line_rims(smooth_field), along_rate, cross_rate)
     smoothed = smooth_field.reshape(own_chan, pixel_count).astype(jnp.bfloat16)
-    return jnp.dot(
-        factor,
-        lax.all_gather(smoothed, "chan", axis=0, tiled=True),
-        preferred_element_type=jnp.float32,
-    )
+    return jnp.dot(factor, launch_floor(smoothed), preferred_element_type=jnp.float32)
 
 
 def solution(mesh):

time: 253 us -> 308 us (1.22); the launches traced: 252 us -> 303 us
  starting transfers between devices: 36.2 us -> 101 us
  waiting for transfers between devices: 170 us -> 128 us
  local copies, waits for them, and re-layouts: 22.4 us -> 63.3 us
  between operations: 13.6 us -> 0.78 us
    all_gather x1 -> x0, waiting for transfers between devices: 69 us -> none  [on_device(): lax.all_gather(smoothed, 'chan', axis=0, tiled=True)]
    ppermute x0 -> x15, starting transfers between devices: none -> 64.7 us  [the longest x7 48.1 us: launch_floor(): response = ppermute(response, axis_name='chan', perm=table)]
    dynamic_update_slice x0 -> x16, local copies, waits for them, and re-layouts: none -> 44.9 us  [the longest x8 22.4 us: launch_floor(): lax.dynamic_update_slice_in_dim(w2, res, (tmp - w) % passed * d_next, axi...]
    ppermute x0 -> x15, waiting for transfers between devices: none -> 27 us  [the longest x8 26.8 us: launch_floor(): res = ppermute(res, 'chan', heap)]
    unnamed x18 -> x30, local copies, waits for them, and re-layouts: 7.56 us -> 0.69 us
  transfers between devices with their start and end apart: 8 -> 22, of which waited for: 5 -> 12; matrix products, arithmetic and copies ran while one was open for 0% -> 15% of each run, Pallas kernels for 0% -> 0%
where the time goes in v1:
time: 308 us; the launch traced here: 303 us
  waiting for transfers between devices  128 us (42%)
  starting transfers between devices  101 us (33%)
  local copies, waits for them, and re-layouts  63.3 us (21%)
  other arithmetic  5.25 us (2%)
  matrix products  4.96 us (2%)
    all_to_all x1, waiting for transfers between devices, on_device(): lax.all_to_all(outgoing, 'swath', split_axis=0, concat_axis=0, tiled=True)  98.4 us
    ppermute x7, starting transfers between devices, launch_floor(): response = ppermute(response, axis_name='chan', perm=table)  48.1 us
    ppermute x8, waiting for transfers between devices, launch_floor(): res = ppermute(res, 'chan', heap)  26.8 us
    dynamic_update_slice x8, local copies, waits for them, and re-layouts, launch_floor(): lax.dynamic_update_slice_in_dim(w2, res, (tmp - w) % passed * d_next, axi...  22.4 us
    dynamic_update_slice x7, local copies, waits for them, and re-layouts, launch_floor(): lax.dynamic_update_slice_in_dim(w2, response, (tmp + w) % passed * d_next...  19.7 us
    all_to_all x1, starting transfers between devices, on_device(): lax.all_to_all(outgoing, 'swath', split_axis=0, concat_axis=0, tiled=True)  16.7 us
    ppermute x8, starting transfers between devices, launch_floor(): res = ppermute(res, 'chan', heap)  16.6 us
    gather x1, local copies, waits for them, and re-layouts, on_device(): grid_profiles[slot_rows]  14.6 us
  transfers between devices with their start and end apart: 22, of which 12 were waited for; matrix products, arithmetic and copies ran while one was open for 15% of the time, Pallas kernels for 0%

profile of v1, /device:TPU:1, one launch (start us, length us, event | category | flops | bytes accessed | tf_op | source)
XLA Modules:
  0.0 303.0 jit_solution(18331730285552362905)
XLA Ops:
  1.5 14.6 %gather_fusion = bf16[4096,256]{1,0:T(8,128)(2,1)S(1)} fusion(bf16[1024,256]{1,0:T(8,128)(2,1)S(1)} %copy-done, s32[4096]{0:T(1024)S(1)} %fusion.29), kind=kCustom, calls=%fused_computation | custom fusion | bytes 4210688 | tf_op jit(solution)/shard_map/gather | solution.py:69
  17.9 16.7 %all-to-all-start = ((bf16[32,128,256]{2,1,0:T(8,128)(2,1)}), bf16[32,128,256]{2,1,0:T(8,128)(2,1)S(1)}, u32[]{:S(2)}, u32[]{:S(2)}) async-start(bf16[32,128,256]{2,1,0:T(8,128)(2,1)} %broadcast_select_fusion), calls=%async_computation | async-start | bytes 4194304 | tf_op jit(solution)/shard_map/all_to_all | solution.py:70
  34.9 98.4 %all-to-all-done = bf16[32,128,256]{2,1,0:T(8,128)(2,1)S(1)} async-done(((bf16[32,128,256]{2,1,0:T(8,128)(2,1)}), bf16[32,128,256]{2,1,0:T(8,128)(2,1)S(1)}, u32[]{:S(2)}, u32[]{:S(2)}) %all-to-all-start) | async-done | bytes 2097184 | tf_op jit(solution)/shard_map/all_to_all | solution.py:70
  135.0 2.8 collective-permute-start
  137.7 4.2 %collective-permute-start.1 = (f32[38,1,128]{2,1,0:T(1,128)S(1)}, f32[38,1,128]{2,1,0:T(1,128)S(1)}, u32[]{:S(2)}, u32[]{:S(2)}) collective-permute-start(f32[38,1,128]{2,1,0:T(1,128)S(1)} %get-tuple-element.15), channel_id=1, source_target_pairs={{0,16},{16,32},{32,48},{48,64},{64,80},{80,96},{96,112},{112,128},... | collective-permute-start | bytes 58376 | tf_op jit(solution)/shard_map/ppermute | solution.py:41
  143.4 1.9 collective-permute-start.2
  145.3 4.2 %collective-permute-start.3 = (f32[38,1,128]{2,1,0:T(1,128)S(1)}, f32[38,1,128]{2,1,0:T(1,128)S(1)}, u32[]{:S(2)}, u32[]{:S(2)}) collective-permute-start(f32[38,1,128]{2,1,0:T(1,128)S(1)} %get-tuple-element.13), channel_id=1, source_target_pairs={{0,16},{16,32},{32,48},{48,64},{64,80},{80,96},{96,112},{112,128},... | collective-permute-start | bytes 58376 | tf_op jit(solution)/shard_map/ppermute | solution.py:41
  151.0 1.9 collective-permute-start.4
  152.9 4.2 %collective-permute-start.5 = (f32[38,1,128]{2,1,0:T(1,128)S(1)}, f32[38,1,128]{2,1,0:T(1,128)S(1)}, u32[]{:S(2)}, u32[]{:S(2)}) collective-permute-start(f32[38,1,128]{2,1,0:T(1,128)S(1)} %get-tuple-element.11), channel_id=1, source_target_pairs={{0,16},{16,32},{32,48},{48,64},{64,80},{80,96},{96,112},{112,128},... | collective-permute-start | bytes 58376 | tf_op jit(solution)/shard_map/ppermute | solution.py:41
  158.8 3.2 %collective-permute-start.6 = (bf16[38,4096]{1,0:T(8,128)(2,1)S(1)}, bf16[38,4096]{1,0:T(8,128)(2,1)S(1)}, u32[]{:S(2)}, u32[]{:S(2)}) collective-permute-start(bf16[38,4096]{1,0:T(8,128)(2,1)S(1)} %bitcast.51), channel_id=1, source_target_pairs={{0,1},{1,2},{2,3},{3,4},{4,5},{5,6},{6,7},{7,8},{8,9},{9,10},{10,1... | collective-permute-start | bytes 933896 | tf_op jit(solution)/shard_map/ppermute | solution.py:26
  162.0 5.6 %collective-permute-start.7 = (bf16[38,4096]{1,0:T(8,128)(2,1)S(1)}, bf16[38,4096]{1,0:T(8,128)(2,1)S(1)}, u32[]{:S(2)}, u32[]{:S(2)}) collective-permute-start(bf16[38,4096]{1,0:T(8,128)(2,1)S(1)} %bitcast.52), channel_id=1, source_target_pairs={{0,15},{1,0},{2,1},{3,2},{4,3},{5,4},{6,5},{7,6},{8,7},{9,8},{10,9... | collective-permute-start | bytes 933896 | tf_op jit(solution)/shard_map/ppermute | solution.py:29
  167.6 4.5 %collective-permute-done.6 = bf16[38,4096]{1,0:T(8,128)(2,1)S(1)} collective-permute-done((bf16[38,4096]{1,0:T(8,128)(2,1)S(1)}, bf16[38,4096]{1,0:T(8,128)(2,1)S(1)}, u32[]{:S(2)}, u32[]{:S(2)}) %collective-permute-start.6) | collective-permute-done | bytes 311328 | tf_op jit(solution)/shard_map/ppermute | solution.py:26
  172.1 1.9 collective-permute-start.8
  174.0 7.0 %collective-permute-start.9 = (bf16[38,4096]{1,0:T(8,128)(2,1)S(1)}, bf16[38,4096]{1,0:T(8,128)(2,1)S(1)}, u32[]{:S(2)}, u32[]{:S(2)}) collective-permute-start(bf16[38,4096]{1,0:T(8,128)(2,1)S(1)} %collective-permute-done.7), channel_id=1, source_target_pairs={{0,15},{1,0},{2,1},{3,2},{4,3},{5,4},{6,5},{7,6},{8,7},{9,8},{10,9... | collective-permute-start | bytes 933896 | tf_op jit(solution)/shard_map/ppermute | solution.py:29
  180.9 5.3 %collective-permute-done.8 = bf16[38,4096]{1,0:T(8,128)(2,1)S(1)} collective-permute-done((bf16[38,4096]{1,0:T(8,128)(2,1)S(1)}, bf16[38,4096]{1,0:T(8,128)(2,1)S(1)}, u32[]{:S(2)}, u32[]{:S(2)}) %collective-permute-start.8) | collective-permute-done | bytes 311328 | tf_op jit(solution)/shard_map/ppermute | solution.py:26
  186.2 1.9 collective-permute-start.10
  188.3 7.2 %collective-permute-start.11 = (bf16[38,4096]{1,0:T(8,128)(2,1)S(1)}, bf16[38,4096]{1,0:T(8,128)(2,1)S(1)}, u32[]{:S(2)}, u32[]{:S(2)}) collective-permute-start(bf16[38,4096]{1,0:T(8,128)(2,1)S(1)} %collective-permute-done.9), channel_id=1, source_target_pairs={{0,15},{1,0},{2,1},{3,2},{4,3},{5,4},{6,5},{7,6},{8,7},{9,8},{10,9... | collective-permute-start | bytes 933896 | tf_op jit(solution)/shard_map/ppermute | solution.py:29
  195.6 4.9 %collective-permute-done.10 = bf16[38,4096]{1,0:T(8,128)(2,1)S(1)} collective-permute-done((bf16[38,4096]{1,0:T(8,128)(2,1)S(1)}, bf16[38,4096]{1,0:T(8,128)(2,1)S(1)}, u32[]{:S(2)}, u32[]{:S(2)}) %collective-permute-start.10) | collective-permute-done | bytes 311328 | tf_op jit(solution)/shard_map/ppermute | solution.py:26
  200.4 1.9 collective-permute-start.12
  202.4 7.3 %collective-permute-start.13 = (bf16[38,4096]{1,0:T(8,128)(2,1)S(1)}, bf16[38,4096]{1,0:T(8,128)(2,1)S(1)}, u32[]{:S(2)}, u32[]{:S(2)}) collective-permute-start(bf16[38,4096]{1,0:T(8,128)(2,1)S(1)} %collective-permute-done.11), channel_id=1, source_target_pairs={{0,15},{1,0},{2,1},{3,2},{4,3},{5,4},{6,5},{7,6},{8,7},{9,8},{10,9... | collective-permute-start | bytes 933896 | tf_op jit(solution)/shard_map/ppermute | solution.py:29
  209.7 4.1 %collective-permute-done.12 = bf16[38,4096]{1,0:T(8,128)(2,1)S(1)} collective-permute-done((bf16[38,4096]{1,0:T(8,128)(2,1)S(1)}, bf16[38,4096]{1,0:T(8,128)(2,1)S(1)}, u32[]{:S(2)}, u32[]{:S(2)}) %collective-permute-start.12) | collective-permute-done | bytes 311328 | tf_op jit(solution)/shard_map/ppermute | solution.py:26
  215.7 7.2 %collective-permute-start.15 = (bf16[38,4096]{1,0:T(8,128)(2,1)S(1)}, bf16[38,4096]{1,0:T(8,128)(2,1)S(1)}, u32[]{:S(2)}, u32[]{:S(2)}) collective-permute-start(bf16[38,4096]{1,0:T(8,128)(2,1)S(1)} %collective-permute-done.13), channel_id=1, source_target_pairs={{0,15},{1,0},{2,1},{3,2},{4,3},{5,4},{6,5},{7,6},{8,7},{9,8},{10,9... | collective-permute-start | bytes 933896 | tf_op jit(solution)/shard_map/ppermute | solution.py:29
  222.9 3.2 %collective-permute-done.14 = bf16[38,4096]{1,0:T(8,128)(2,1)S(1)} collective-permute-done((bf16[38,4096]{1,0:T(8,128)(2,1)S(1)}, bf16[38,4096]{1,0:T(8,128)(2,1)S(1)}, u32[]{:S(2)}, u32[]{:S(2)}) %collective-permute-start.14) | collective-permute-done | bytes 311328 | tf_op jit(solution)/shard_map/ppermute | solution.py:26
  226.1 1.9 collective-permute-start.16
  228.1 7.1 %collective-permute-start.17 = (bf16[38,4096]{1,0:T(8,128)(2,1)S(1)}, bf16[38,4096]{1,0:T(8,128)(2,1)}, u32[]{:S(2)}, u32[]{:S(2)}) collective-permute-start(bf16[38,4096]{1,0:T(8,128)(2,1)S(1)} %collective-permute-done.15), channel_id=1, source_target_pairs={{0,15},{1,0},{2,1},{3,2},{4,3},{5,4},{6,5},{7,6},{8,7},{9,8},{10,9... | collective-permute-start | bytes 933896 | tf_op jit(solution)/shard_map/ppermute | solution.py:29
  235.1 2.4 collective-permute-done.16
  237.6 1.9 collective-permute-start.18
  239.5 6.9 %collective-permute-start.19 = (bf16[38,4096]{1,0:T(8,128)(2,1)}, bf16[38,4096]{1,0:T(8,128)(2,1)}, u32[]{:S(2)}, u32[]{:S(2)}) collective-permute-start(bf16[38,4096]{1,0:T(8,128)(2,1)} %collective-permute-done.17), channel_id=1, source_target_pairs={{0,15},{1,0},{2,1},{3,2},{4,3},{5,4},{6,5},{7,6},{8,7},{9,8},{10,9... | collective-permute-start | bytes 933896 | tf_op jit(solution)/shard_map/ppermute | solution.py:29
  246.4 2.4 collective-permute-done.18
  248.8 1.9 collective-permute-start.20
  251.0 2.9 broadcast_in_dim.20
  253.9 2.8 dynamic_update_slice.48
  256.7 2.7 dynamic_update_slice.49
  259.4 2.8 dynamic_update_slice.50
  262.2 2.8 dynamic_update_slice.51
  265.0 2.7 dynamic_update_slice.52
  267.8 2.8 dynamic_update_slice.53
  270.5 2.8 dynamic_update_slice.54
  273.3 2.8 dynamic_update_slice.55
  276.0 2.8 dynamic_update_slice.56
  278.8 2.8 dynamic_update_slice.57
  281.6 2.8 dynamic_update_slice.58
  284.3 2.8 dynamic_update_slice.59
  287.1 2.9 dynamic_update_slice.60
  290.0 2.9 dynamic_update_slice.61
  292.9 2.9 dynamic_update_slice.62
  295.9 2.9 dynamic_update_slice.63
  298.8 4.2 %convolution_bitcast_fusion.1 = f32[38,4096]{1,0:T(8,128)} fusion(bf16[608,4096]{1,0:T(8,128)(2,1)} %dynamic_update_slice.63, bf16[38,608]{1,0:T(8,128)(2,1)S(1)} %copy-done.9), kind=kOutput, calls=%fused_computation.2 | convolution fusion | flops 189267968 | bytes 5649536 | tf_op jit(solution)/shard_map/dot_general | solution.py:85
  (60 shorter events, 11.7 us)
Async XLA Ops:
  0.0 1.5 copy-start
  16.1 18.5 %copy-start.7 = (bf16[38,4096]{1,0:T(8,128)(2,1)S(1)}, bf16[38,4096]{1,0:T(8,128)(2,1)}, u32[]{:S(2)}) copy-start(bf16[38,4096]{1,0:T(8,128)(2,1)} %param.13) | copy-start | bytes 933892
  16.1 18.7 %copy-start.11 = (s32[128]{0:T(128)S(1)}, s32[128]{0:T(128)}, u32[]{:S(2)}) copy-start(s32[128]{0:T(128)} %param.11) | copy-start | bytes 1540
  16.2 117.1 %copy-start.8 = (bf16[3,256,38]{1,2,0:T(8,128)(2,1)S(1)}, bf16[3,256,38]{1,2,0:T(8,128)(2,1)}, u32[]{:S(2)}) copy-start(bf16[3,256,38]{1,2,0:T(8,128)(2,1)} %param.12) | copy-start | bytes 175108
  17.9 115.4 %all-to-all-start = ((bf16[32,128,256]{2,1,0:T(8,128)(2,1)}), bf16[32,128,256]{2,1,0:T(8,128)(2,1)S(1)}, u32[]{:S(2)}, u32[]{:S(2)}) async-start(bf16[32,128,256]{2,1,0:T(8,128)(2,1)} %broadcast_select_fusion), calls=%async_computation | async-start | bytes 4194304 | tf_op jit(solution)/shard_map/all_to_all | solution.py:70
  134.0 7.9 %copy-start.10 = (f32[2,38]{1,0:T(2,128)S(1)}, f32[2,38]{1,0:T(2,128)}, u32[]{:S(2)}) copy-start(f32[2,38]{1,0:T(2,128)} %param.14) | copy-start | bytes 916
  135.0 7.0 %collective-permute-start = (f32[38,1,128]{2,1,0:T(1,128)S(1)}, f32[38,1,128]{2,1,0:T(1,128)S(1)}, u32[]{:S(2)}, u32[]{:S(2)}) collective-permute-start(f32[38,1,128]{2,1,0:T(1,128)S(1)} %get-tuple-element.14), channel_id=1, source_target_pairs={{16,0},{32,16},{48,32},{64,48},{80,64},{96,80},{112,96},{128,112},... | collective-permute-start | bytes 58376 | tf_op jit(solution)/shard_map/ppermute | solution.py:44
  137.7 5.1 %collective-permute-start.1 = (f32[38,1,128]{2,1,0:T(1,128)S(1)}, f32[38,1,128]{2,1,0:T(1,128)S(1)}, u32[]{:S(2)}, u32[]{:S(2)}) collective-permute-start(f32[38,1,128]{2,1,0:T(1,128)S(1)} %get-tuple-element.15), channel_id=1, source_target_pairs={{0,16},{16,32},{32,48},{48,64},{64,80},{80,96},{96,112},{112,128},... | collective-permute-start | bytes 58376 | tf_op jit(solution)/shard_map/ppermute | solution.py:41
  143.4 6.1 %collective-permute-start.2 = (f32[38,1,128]{2,1,0:T(1,128)S(1)}, f32[38,1,128]{2,1,0:T(1,128)S(1)}, u32[]{:S(2)}, u32[]{:S(2)}) collective-permute-start(f32[38,1,128]{2,1,0:T(1,128)S(1)} %get-tuple-element.12), channel_id=1, source_target_pairs={{16,0},{32,16},{48,32},{64,48},{80,64},{96,80},{112,96},{128,112},... | collective-permute-start | bytes 58376 | tf_op jit(solution)/shard_map/ppermute | solution.py:44
  145.3 5.1 %collective-permute-start.3 = (f32[38,1,128]{2,1,0:T(1,128)S(1)}, f32[38,1,128]{2,1,0:T(1,128)S(1)}, u32[]{:S(2)}, u32[]{:S(2)}) collective-permute-start(f32[38,1,128]{2,1,0:T(1,128)S(1)} %get-tuple-element.13), channel_id=1, source_target_pairs={{0,16},{16,32},{32,48},{48,64},{64,80},{80,96},{96,112},{112,128},... | collective-permute-start | bytes 58376 | tf_op jit(solution)/shard_map/ppermute | solution.py:41
  151.0 6.1 %collective-permute-start.4 = (f32[38,1,128]{2,1,0:T(1,128)S(1)}, f32[38,1,128]{2,1,0:T(1,128)S(1)}, u32[]{:S(2)}, u32[]{:S(2)}) collective-permute-start(f32[38,1,128]{2,1,0:T(1,128)S(1)} %get-tuple-element.10), channel_id=1, source_target_pairs={{16,0},{32,16},{48,32},{64,48},{80,64},{96,80},{112,96},{128,112},... | collective-permute-start | bytes 58376 | tf_op jit(solution)/shard_map/ppermute | solution.py:44
  152.9 5.1 %collective-permute-start.5 = (f32[38,1,128]{2,1,0:T(1,128)S(1)}, f32[38,1,128]{2,1,0:T(1,128)S(1)}, u32[]{:S(2)}, u32[]{:S(2)}) collective-permute-start(f32[38,1,128]{2,1,0:T(1,128)S(1)} %get-tuple-element.11), channel_id=1, source_target_pairs={{0,16},{16,32},{32,48},{48,64},{64,80},{80,96},{96,112},{112,128},... | collective-permute-start | bytes 58376 | tf_op jit(solution)/shard_map/ppermute | solution.py:41
  158.8 13.3 %collective-permute-start.6 = (bf16[38,4096]{1,0:T(8,128)(2,1)S(1)}, bf16[38,4096]{1,0:T(8,128)(2,1)S(1)}, u32[]{:S(2)}, u32[]{:S(2)}) collective-permute-start(bf16[38,4096]{1,0:T(8,128)(2,1)S(1)} %bitcast.51), channel_id=1, source_target_pairs={{0,1},{1,2},{2,3},{3,4},{4,5},{5,6},{6,7},{7,8},{8,9},{9,10},{10,1... | collective-permute-start | bytes 933896 | tf_op jit(solution)/shard_map/ppermute | solution.py:26
  162.0 12.0 %collective-permute-start.7 = (bf16[38,4096]{1,0:T(8,128)(2,1)S(1)}, bf16[38,4096]{1,0:T(8,128)(2,1)S(1)}, u32[]{:S(2)}, u32[]{:S(2)}) collective-permute-start(bf16[38,4096]{1,0:T(8,128)(2,1)S(1)} %bitcast.52), channel_id=1, source_target_pairs={{0,15},{1,0},{2,1},{3,2},{4,3},{5,4},{6,5},{7,6},{8,7},{9,8},{10,9... | collective-permute-start | bytes 933896 | tf_op jit(solution)/shard_map/ppermute | solution.py:29
  172.1 14.2 %collective-permute-start.8 = (bf16[38,4096]{1,0:T(8,128)(2,1)S(1)}, bf16[38,4096]{1,0:T(8,128)(2,1)S(1)}, u32[]{:S(2)}, u32[]{:S(2)}) collective-permute-start(bf16[38,4096]{1,0:T(8,128)(2,1)S(1)} %collective-permute-done.6), channel_id=1, source_target_pairs={{0,1},{1,2},{2,3},{3,4},{4,5},{5,6},{6,7},{7,8},{8,9},{9,10},{10,1... | collective-permute-start | bytes 933896 | tf_op jit(solution)/shard_map/ppermute | solution.py:26
  174.0 14.3 %collective-permute-start.9 = (bf16[38,4096]{1,0:T(8,128)(2,1)S(1)}, bf16[38,4096]{1,0:T(8,128)(2,1)S(1)}, u32[]{:S(2)}, u32[]{:S(2)}) collective-permute-start(bf16[38,4096]{1,0:T(8,128)(2,1)S(1)} %collective-permute-done.7), channel_id=1, source_target_pairs={{0,15},{1,0},{2,1},{3,2},{4,3},{5,4},{6,5},{7,6},{8,7},{9,8},{10,9... | collective-permute-start | bytes 933896 | tf_op jit(solution)/shard_map/ppermute | solution.py:29
  186.2 14.2 %collective-permute-start.10 = (bf16[38,4096]{1,0:T(8,128)(2,1)S(1)}, bf16[38,4096]{1,0:T(8,128)(2,1)S(1)}, u32[]{:S(2)}, u32[]{:S(2)}) collective-permute-start(bf16[38,4096]{1,0:T(8,128)(2,1)S(1)} %collective-permute-done.8), channel_id=1, source_target_pairs={{0,1},{1,2},{2,3},{3,4},{4,5},{5,6},{6,7},{7,8},{8,9},{9,10},{10,1... | collective-permute-start | bytes 933896 | tf_op jit(solution)/shard_map/ppermute | solution.py:26
  188.3 14.0 %collective-permute-start.11 = (bf16[38,4096]{1,0:T(8,128)(2,1)S(1)}, bf16[38,4096]{1,0:T(8,128)(2,1)S(1)}, u32[]{:S(2)}, u32[]{:S(2)}) collective-permute-start(bf16[38,4096]{1,0:T(8,128)(2,1)S(1)} %collective-permute-done.9), channel_id=1, source_target_pairs={{0,15},{1,0},{2,1},{3,2},{4,3},{5,4},{6,5},{7,6},{8,7},{9,8},{10,9... | collective-permute-start | bytes 933896 | tf_op jit(solution)/shard_map/ppermute | solution.py:29
  200.4 13.3 %collective-permute-start.12 = (bf16[38,4096]{1,0:T(8,128)(2,1)S(1)}, bf16[38,4096]{1,0:T(8,128)(2,1)S(1)}, u32[]{:S(2)}, u32[]{:S(2)}) collective-permute-start(bf16[38,4096]{1,0:T(8,128)(2,1)S(1)} %collective-permute-done.10), channel_id=1, source_target_pairs={{0,1},{1,2},{2,3},{3,4},{4,5},{5,6},{6,7},{7,8},{8,9},{9,10},{10,1... | collective-permute-start | bytes 933896 | tf_op jit(solution)/shard_map/ppermute | solution.py:26
  202.4 13.3 %collective-permute-start.13 = (bf16[38,4096]{1,0:T(8,128)(2,1)S(1)}, bf16[38,4096]{1,0:T(8,128)(2,1)S(1)}, u32[]{:S(2)}, u32[]{:S(2)}) collective-permute-start(bf16[38,4096]{1,0:T(8,128)(2,1)S(1)} %collective-permute-done.11), channel_id=1, source_target_pairs={{0,15},{1,0},{2,1},{3,2},{4,3},{5,4},{6,5},{7,6},{8,7},{9,8},{10,9... | collective-permute-start | bytes 933896 | tf_op jit(solution)/shard_map/ppermute | solution.py:29
  213.7 12.4 %collective-permute-start.14 = (bf16[38,4096]{1,0:T(8,128)(2,1)S(1)}, bf16[38,4096]{1,0:T(8,128)(2,1)S(1)}, u32[]{:S(2)}, u32[]{:S(2)}) collective-permute-start(bf16[38,4096]{1,0:T(8,128)(2,1)S(1)} %collective-permute-done.12), channel_id=1, source_target_pairs={{0,1},{1,2},{2,3},{3,4},{4,5},{5,6},{6,7},{7,8},{8,9},{9,10},{10,1... | collective-permute-start | bytes 933896 | tf_op jit(solution)/shard_map/ppermute | solution.py:26
  215.7 12.4 %collective-permute-start.15 = (bf16[38,4096]{1,0:T(8,128)(2,1)S(1)}, bf16[38,4096]{1,0:T(8,128)(2,1)S(1)}, u32[]{:S(2)}, u32[]{:S(2)}) collective-permute-start(bf16[38,4096]{1,0:T(8,128)(2,1)S(1)} %collective-permute-done.13), channel_id=1, source_target_pairs={{0,15},{1,0},{2,1},{3,2},{4,3},{5,4},{6,5},{7,6},{8,7},{9,8},{10,9... | collective-permute-start | bytes 933896 | tf_op jit(solution)/shard_map/ppermute | solution.py:29
  226.1 1.9 copy-start.1
  226.1 11.4 %collective-permute-start.16 = (bf16[38,4096]{1,0:T(8,128)(2,1)S(1)}, bf16[38,4096]{1,0:T(8,128)(2,1)S(1)}, u32[]{:S(2)}, u32[]{:S(2)}) collective-permute-start(bf16[38,4096]{1,0:T(8,128)(2,1)S(1)} %collective-permute-done.14), channel_id=1, source_target_pairs={{0,1},{1,2},{2,3},{3,4},{4,5},{5,6},{6,7},{7,8},{8,9},{9,10},{10,1... | collective-permute-start | bytes 933896 | tf_op jit(solution)/shard_map/ppermute | solution.py:26
  228.0 9.5 %copy-start.3 = (bf16[38,4096]{1,0:T(8,128)(2,1)}, bf16[38,4096]{1,0:T(8,128)(2,1)S(1)}, u32[]{:S(2)}) copy-start(bf16[38,4096]{1,0:T(8,128)(2,1)S(1)} %collective-permute-done.15) | copy-start | bytes 933892
  228.1 11.4 %collective-permute-start.17 = (bf16[38,4096]{1,0:T(8,128)(2,1)S(1)}, bf16[38,4096]{1,0:T(8,128)(2,1)}, u32[]{:S(2)}, u32[]{:S(2)}) collective-permute-start(bf16[38,4096]{1,0:T(8,128)(2,1)S(1)} %collective-permute-done.15), channel_id=1, source_target_pairs={{0,15},{1,0},{2,1},{3,2},{4,3},{5,4},{6,5},{7,6},{8,7},{9,8},{10,9... | collective-permute-start | bytes 933896 | tf_op jit(solution)/shard_map/ppermute | solution.py:29
  237.5 1.9 copy-start.5
  237.6 11.2 %collective-permute-start.18 = (bf16[38,4096]{1,0:T(8,128)(2,1)S(1)}, bf16[38,4096]{1,0:T(8,128)(2,1)}, u32[]{:S(2)}, u32[]{:S(2)}) collective-permute-start(bf16[38,4096]{1,0:T(8,128)(2,1)S(1)} %collective-permute-done.16), channel_id=1, source_target_pairs={{0,1},{1,2},{2,3},{3,4},{4,5},{5,6},{6,7},{7,8},{8,9},{9,10},{10,1... | collective-permute-start | bytes 933896 | tf_op jit(solution)/shard_map/ppermute | solution.py:26
  239.5 53.5 %collective-permute-start.19 = (bf16[38,4096]{1,0:T(8,128)(2,1)}, bf16[38,4096]{1,0:T(8,128)(2,1)}, u32[]{:S(2)}, u32[]{:S(2)}) collective-permute-start(bf16[38,4096]{1,0:T(8,128)(2,1)} %collective-permute-done.17), channel_id=1, source_target_pairs={{0,15},{1,0},{2,1},{3,2},{4,3},{5,4},{6,5},{7,6},{8,7},{9,8},{10,9... | collective-permute-start | bytes 933896 | tf_op jit(solution)/shard_map/ppermute | solution.py:29
  248.8 47.1 %collective-permute-start.20 = (bf16[38,4096]{1,0:T(8,128)(2,1)}, bf16[38,4096]{1,0:T(8,128)(2,1)}, u32[]{:S(2)}, u32[]{:S(2)}) collective-permute-start(bf16[38,4096]{1,0:T(8,128)(2,1)} %collective-permute-done.18), channel_id=1, source_target_pairs={{0,1},{1,2},{2,3},{3,4},{4,5},{5,6},{6,7},{7,8},{8,9},{9,10},{10,1... | collective-permute-start | bytes 933896 | tf_op jit(solution)/shard_map/ppermute | solution.py:26
  256.7 22.1 %copy-start.2 = (bf16[38,4096]{1,0:T(8,128)(2,1)S(1)}, bf16[38,4096]{1,0:T(8,128)(2,1)}, u32[]{:S(2)}) copy-start(bf16[38,4096]{1,0:T(8,128)(2,1)} %copy-done.1) | copy-start | bytes 933892
  256.7 42.1 %copy-start.9 = (bf16[38,608]{1,0:T(8,128)(2,1)S(1)}, bf16[38,608]{1,0:T(8,128)(2,1)}, u32[]{:S(2)}) copy-start(bf16[38,608]{1,0:T(8,128)(2,1)} %param.15) | copy-start | bytes 138628
  259.4 22.1 %copy-start.4 = (bf16[38,4096]{1,0:T(8,128)(2,1)S(1)}, bf16[38,4096]{1,0:T(8,128)(2,1)}, u32[]{:S(2)}) copy-start(bf16[38,4096]{1,0:T(8,128)(2,1)} %copy-done.3) | copy-start | bytes 933892
  262.2 22.1 %copy-start.6 = (bf16[38,4096]{1,0:T(8,128)(2,1)S(1)}, bf16[38,4096]{1,0:T(8,128)(2,1)}, u32[]{:S(2)}) copy-start(bf16[38,4096]{1,0:T(8,128)(2,1)} %copy-done.5) | copy-start | bytes 933892
